TPU v7x, 128 devices: a whole 4x4x4 slice. The times are simulated.
128 devices in a mesh: grp: 2 (over core), row: 8 (over x_lo, y), col: 8 (over z, x_hi).
Axes of the slice: x: 4 (x_hi: 2, x_lo: 2; x = x_hi * 2 + x_lo), y: 4, z: 4, core: 2. Of those that a mesh axis runs over, the one named last changes fastest.
Arguments:
- conserved: float32 [5, 512, 4096], P(None, 'row', 'col'), may hold values from -1 to 5.5, as said below
- displacement: float32 [2, 512, 4096], P(None, ('row', 'col')), may hold values from -0.3 to 0.3
Outputs:
- group_fields: float32 [2, 5, 512, 4096], P('grp', None, 'row', 'col')
Inputs may be any that keep to these rules, and one draw needn't show every extreme that they name: `conserved`: per cell: density and pressure (0.4 times the energy minus the kinetic energy) lie between 1 and 2, both speeds between -0.5 and 0.5, the tracer fraction between 0 and 1.
All inputs are finite; a program needn't handle non-finite values.
Results may differ from a plain program's by a relative error of at most 0.0003.
Values sent between devices are 32-bit elements; how exact they have to be, the bound alone decides.
No kernel may reach another device: no remote copies, remote signals or barrier semaphores. Data moves between devices by JAX's collectives and lax.ppermute only.
A program may use at most 64 MiB of HBM per device.

v0:
```python
import jax
import jax.numpy as jnp
from jax import lax
from jax.sharding import PartitionSpec as P

STEPS = 2
SWEEPS = 4
HEAT_RATIO = 1.4
TIME_STEP = 0.08
GRADIENT_GAIN = 8.0
MONITOR_GAIN = 0.2
RELAXATION = 0.5


def partner(block, axis, apart):
    count = lax.axis_size(axis)
    route = []
    for low in range(count):
        high = low | 1 << apart
        if high != low and high < count:
            route += [(low, high), (high, low)]
    return lax.ppermute(block, axis, route)


def with_halo(cells, sides, width):
    for axis, dim in sides:
        count = lax.axis_size(axis)
        head = lax.slice_in_dim(cells, 0, width, axis=dim)
        tail = lax.slice_in_dim(cells, cells.shape[dim] - width, cells.shape[dim], axis=dim)
        cells = jnp.concatenate(
            [
                lax.ppermute(tail, axis, [(i, (i + 1) % count) for i in range(count)]),
                cells,
                lax.ppermute(head, axis, [((i + 1) % count, i) for i in range(count)]),
            ],
            axis=dim,
        )
    return cells


def minmod(lower_diff, upper_diff):
    smaller = jnp.where(jnp.abs(lower_diff) < jnp.abs(upper_diff), lower_diff, upper_diff)
    return jnp.where(lower_diff * upper_diff > 0.0, smaller, 0.0)


def primitives(fields):
    density = fields[0]
    speed_x = fields[1] / density
    speed_y = fields[2] / density
    pressure = (HEAT_RATIO - 1.0) * (fields[3] - 0.5 * (fields[1] * speed_x + fields[2] * speed_y))
    tracer = fields[4] / density
    return jnp.stack([density, speed_x, speed_y, pressure, tracer])


def normal_flux(states, normal_x, normal_y):
    density, speed_x, speed_y, pressure, tracer = (
        states[0],
        states[1],
        states[2],
        states[3],
        states[4],
    )
    normal_speed = speed_x * normal_x + speed_y * normal_y
    energy = pressure / (HEAT_RATIO - 1.0) + 0.5 * density * (speed_x * speed_x + speed_y * speed_y)
    conserved = jnp.stack([density, density * speed_x, density * speed_y, energy, density * tracer])
    flux_terms = jnp.stack(
        [
            density * normal_speed,
            density * speed_x * normal_speed + pressure * normal_x,
            density * speed_y * normal_speed + pressure * normal_y,
            (energy + pressure) * normal_speed,
            density * tracer * normal_speed,
        ]
    )
    wave_speed = jnp.abs(normal_speed) + jnp.sqrt(HEAT_RATIO * pressure / density) * jnp.sqrt(
        normal_x * normal_x + normal_y * normal_y
    )
    return (conserved, flux_terms, wave_speed)


def rusanov(left_state, right_state, normal_x, normal_y):
    cons_left, flux_left, wave_left = normal_flux(left_state, normal_x, normal_y)
    cons_right, flux_right, wave_right = normal_flux(right_state, normal_x, normal_y)
    wave_speed = jnp.maximum(wave_left, wave_right)
    return 0.5 * (flux_left + flux_right) - 0.5 * wave_speed * (cons_right - cons_left)


def face_states(primitive, along_axis):
    extent = primitive.shape[along_axis]
    differences = lax.slice_in_dim(primitive, 1, extent, axis=along_axis) - lax.slice_in_dim(
        primitive, 0, extent - 1, axis=along_axis
    )
    slopes = minmod(
        lax.slice_in_dim(differences, 0, extent - 2, axis=along_axis),
        lax.slice_in_dim(differences, 1, extent - 1, axis=along_axis),
    )
    left_state = lax.slice_in_dim(
        primitive, 1, extent - 2, axis=along_axis
    ) + 0.5 * lax.slice_in_dim(slopes, 0, extent - 3, axis=along_axis)
    right_state = lax.slice_in_dim(
        primitive, 2, extent - 1, axis=along_axis
    ) - 0.5 * lax.slice_in_dim(slopes, 1, extent - 2, axis=along_axis)
    return (left_state, right_state)


def advance(extended):
    primitive = primitives(extended[:5])
    shift_x = extended[5]
    shift_y = extended[6]
    slope_x_col = 1.0 + 0.5 * (shift_x[1:-1, 2:] - shift_x[1:-1, :-2])
    slope_x_row = 0.5 * (shift_x[2:, 1:-1] - shift_x[:-2, 1:-1])
    slope_y_col = 0.5 * (shift_y[1:-1, 2:] - shift_y[1:-1, :-2])
    slope_y_row = 1.0 + 0.5 * (shift_y[2:, 1:-1] - shift_y[:-2, 1:-1])
    normal_x = 0.5 * (slope_y_row[1:-1, :-1] + slope_y_row[1:-1, 1:])
    normal_y = -0.5 * (slope_x_row[1:-1, :-1] + slope_x_row[1:-1, 1:])
    left_state, right_state = face_states(primitive[:, 2:-2, :], 2)
    col_flux = rusanov(left_state, right_state, normal_x, normal_y)
    normal_x = -0.5 * (slope_y_col[:-1, 1:-1] + slope_y_col[1:, 1:-1])
    normal_y = 0.5 * (slope_x_col[:-1, 1:-1] + slope_x_col[1:, 1:-1])
    left_state, right_state = face_states(primitive[:, :, 2:-2], 1)
    row_flux = rusanov(left_state, right_state, normal_x, normal_y)
    jacobian = (
        slope_x_col[1:-1, 1:-1] * slope_y_row[1:-1, 1:-1]
        - slope_x_row[1:-1, 1:-1] * slope_y_col[1:-1, 1:-1]
    )
    change = col_flux[:, :, 1:] - col_flux[:, :, :-1] + (row_flux[:, 1:, :] - row_flux[:, :-1, :])
    return extended[:5, 2:-2, 2:-2] - TIME_STEP / jacobian * change


def monitor(density, pressure):
    density_col = 0.5 * (density[1:-1, 2:] - density[1:-1, :-2])
    density_row = 0.5 * (density[2:, 1:-1] - density[:-2, 1:-1])
    pressure_col = 0.5 * (pressure[1:-1, 2:] - pressure[1:-1, :-2])
    pressure_row = 0.5 * (pressure[2:, 1:-1] - pressure[:-2, 1:-1])
    strength = GRADIENT_GAIN * (
        density_col * density_col
        + density_row * density_row
        + pressure_col * pressure_col
        + pressure_row * pressure_row
    )
    return 1.0 + MONITOR_GAIN * strength / (1.0 + strength)


def jacobi(shifts, weight):
    center = weight[1:-1, 1:-1]
    east_face = 0.5 * (center + weight[1:-1, 2:])
    west_face = 0.5 * (center + weight[1:-1, :-2])
    north_face = 0.5 * (center + weight[2:, 1:-1])
    south_face = 0.5 * (center + weight[:-2, 1:-1])
    face_total = east_face + west_face + north_face + south_face
    middle = shifts[:, 1:-1, 1:-1]
    beside_all = (
        east_face * shifts[:, 1:-1, 2:]
        + west_face * shifts[:, 1:-1, :-2]
        + north_face * shifts[:, 2:, 1:-1]
        + south_face * shifts[:, :-2, 1:-1]
    )
    source = jnp.stack([east_face - west_face, north_face - south_face])
    target = (beside_all + source) / face_total
    return middle + RELAXATION * (target - middle)


def pair_of(fields):
    primitive = primitives(fields)
    return jnp.stack([primitive[0], primitive[3]])


def on_device(conserved, displacement):
    on_mesh = lax.axis_index("grp") == 1
    column_count = lax.axis_size("col")
    block_rows = conserved.shape[1]
    block_cols = conserved.shape[2]
    slab_rows = displacement.shape[1]

    def to_pieces_block(values):
        return values.reshape(values.shape[0], column_count, slab_rows, block_cols)

    def to_pieces_slab(values):
        return values.reshape(values.shape[0], slab_rows, column_count, block_cols).transpose(
            0, 2, 1, 3
        )

    def from_pieces_block(values):
        return values.reshape(values.shape[0], block_rows, block_cols)

    def from_pieces_slab(values):
        return values.transpose(0, 2, 1, 3).reshape(
            values.shape[0], slab_rows, column_count * block_cols
        )

    def regroup(values):
        return lax.all_to_all(values, "col", split_axis=1, concat_axis=1, tiled=True)

    def only_mesh(worker, fallback, operands):
        return lax.cond(on_mesh, lambda packed: worker(*packed), lambda packed: fallback, operands)

    def slab_extend(values, margin):
        extended = with_halo(values, ((("row", "col"), 1),), margin)
        return jnp.concatenate(
            [extended[:, :, -margin:], extended, extended[:, :, :margin]], axis=2
        )

    pairs_block = pair_of(conserved)
    arrived = regroup(
        jnp.where(on_mesh, to_pieces_block(pairs_block), to_pieces_slab(displacement))
    )
    shifts_block = from_pieces_block(arrived)
    pairs_mesh = from_pieces_slab(arrived)
    shifts_mesh = displacement
    current = conserved
    previous = shifts_mesh
    weight = jnp.zeros(shifts_mesh.shape[1:], jnp.float32)
    for step_index in range(STEPS):
        physics_extended = with_halo(
            jnp.concatenate([current, shifts_block]), (("row", 1), ("col", 2)), 2
        )
        only_fallback = current
        new_state = lax.cond(
            on_mesh,
            lambda packed: only_fallback,
            lambda packed: advance(*packed),
            (physics_extended,),
        )
        shifts = shifts_mesh
        mesh_extended = slab_extend(jnp.concatenate([pairs_mesh, shifts]), 2)
        blank = jnp.zeros((mesh_extended.shape[1] - 2, mesh_extended.shape[2] - 2), jnp.float32)
        weight_cycle = only_mesh(monitor, blank, (mesh_extended[0], mesh_extended[1]))
        rim_shifts = mesh_extended[2:4, 1:-1, 1:-1]
        for sweep_index in range(SWEEPS):
            if sweep_index > 0:
                rim_shifts = slab_extend(shifts, 1)
            shifts = only_mesh(jacobi, shifts, (rim_shifts, weight_cycle))
        mesh_weight = weight_cycle[1:-1, 1:-1]
        weight = mesh_weight
        if step_index + 1 < STEPS:
            new_pairs = pair_of(new_state)
            outgoing = jnp.where(on_mesh, to_pieces_slab(shifts), to_pieces_block(new_pairs))
            arrived = partner(regroup(outgoing), "grp", 0)
            shifts_block = from_pieces_block(arrived)
            pairs_mesh = from_pieces_slab(arrived)
        previous = shifts_mesh
        shifts_mesh = shifts
        current = new_state
    mesh_fields = jnp.stack(
        [
            shifts_mesh[0],
            shifts_mesh[1],
            (shifts_mesh[0] - previous[0]) / TIME_STEP,
            (shifts_mesh[1] - previous[1]) / TIME_STEP,
            weight,
        ]
    )
    mesh_fields = from_pieces_block(regroup(to_pieces_slab(mesh_fields)))
    return jnp.where(on_mesh, mesh_fields, current)[None]


def solution(mesh):
    placed = (P(None, "row", "col"), P(None, ("row", "col"), None))
    return jax.shard_map(
        on_device,
        mesh=mesh,
        in_specs=placed,
        out_specs=P("grp", None, "row", "col"),
        check_vma=False,
    )
```

profile of v0, /device:TPU:0, one launch (start us, length us, event | category | flops | bytes accessed | tf_op | source)
XLA Modules:
  0.0 186.9 jit_solution(14474896401639339898)
XLA Ops:
  2.2 16.5 %all_to_all.15 = f32[2,8,8,512]{3,2,0,1:T(8,128)S(1)} all-to-all(f32[2,8,8,512]{3,2,0,1:T(8,128)S(1)} %copy.13), channel_id=1, replica_groups=mesh['grp'=2,'row'=8,'col'=8] {'col'}, dimensions={1} | all-to-all | bytes 524288 | tf_op jit(solution)/shard_map/all_to_all | solution.py:192
  18.8 3.7 %collective-permute-start.1 = (f32[4,2,4096]{2,1,0:T(2,128)S(1)}, f32[4,2,4096]{2,1,0:T(2,128)S(1)}, u32[]{:S(2)}, u32[]{:S(2)}) collective-permute-start(f32[4,2,4096]{2,1,0:T(2,128)S(1)} %get-tuple-element.352), channel_id=1, source_target_pairs={{1,0},{2,1},{3,2},{4,3},{5,4},{6,5},{7,6},{8,7},{9,8},{10,9},{11,1... | collective-permute-start | bytes 393224 | tf_op jit(solution)/shard_map/ppermute | solution.py:34
  22.6 3.0 %collective-permute-start.9 = (f32[7,2,512]{2,1,0:T(2,128)S(1)}, f32[7,2,512]{2,1,0:T(2,128)S(1)}, u32[]{:S(2)}, u32[]{:S(2)}) collective-permute-start(f32[7,2,512]{2,1,0:T(2,128)S(1)} %get-tuple-element.330), channel_id=1, source_target_pairs={{8,0},{16,8},{24,16},{32,24},{40,32},{48,40},{56,48},{0,56},{9,1},... | collective-permute-start | bytes 86024 | tf_op jit(solution)/shard_map/ppermute | solution.py:34
  26.5 6.7 %collective-permute-done = f32[4,2,4096]{2,1,0:T(2,128)S(1)} collective-permute-done((f32[4,2,4096]{2,1,0:T(2,128)S(1)}, f32[4,2,4096]{2,1,0:T(2,128)S(1)}, u32[]{:S(2)}, u32[]{:S(2)}) %collective-permute-start) | collective-permute-done | bytes 131104 | tf_op jit(solution)/shard_map/ppermute | solution.py:32
  43.5 7.2 %collective-permute-done.3 = f32[2,1,4096]{2,1,0:T(1,128)S(1)} collective-permute-done((f32[2,1,4096]{2,1,0:T(1,128)S(1)}, f32[2,1,4096]{2,1,0:T(1,128)S(1)}, u32[]{:S(2)}, u32[]{:S(2)}) %collective-permute-start.3) | collective-permute-done | bytes 32800 | tf_op jit(solution)/shard_map/ppermute | solution.py:34
  50.7 3.7 %collective-permute-done.2 = f32[2,1,4096]{2,1,0:T(1,128)S(1)} collective-permute-done((f32[2,1,4096]{2,1,0:T(1,128)S(1)}, f32[2,1,4096]{2,1,0:T(1,128)S(1)}, u32[]{:S(2)}, u32[]{:S(2)}) %collective-permute-start.2) | collective-permute-done | bytes 32800 | tf_op jit(solution)/shard_map/ppermute | solution.py:32
  54.9 4.3 %collective-permute-start.5 = (f32[2,1,4096]{2,1,0:T(1,128)S(1)}, f32[2,1,4096]{2,1,0:T(1,128)S(1)}, u32[]{:S(2)}, u32[]{:S(2)}) collective-permute-start(f32[2,1,4096]{2,1,0:T(1,128)S(1)} %get-tuple-element.362), channel_id=1, source_target_pairs={{1,0},{2,1},{3,2},{4,3},{5,4},{6,5},{7,6},{8,7},{9,8},{10,9},{11,1... | collective-permute-start | bytes 98312 | tf_op jit(solution)/shard_map/ppermute | solution.py:34
  60.9 6.8 %conditional.17 = (f32[5,64,512]{2,1,0:T(8,128)S(1)}) conditional(s32[]{:T(128)} %convert_element_type.2, (f32[7,68,516]{2,1,0:T(8,128)S(1)}, f32[5,64,512]{2,1,0:T(8,128)S(1)}) %tuple.239, f32[5,64,512]{2,1,0:T(8,128)S(1)} %copy-done), branch_computations={%region_10.11_spmd, %region_11.12_spmd} | conditional | flops 12940432 | bytes 60802312 | solution.py:218
  69.0 6.7 %collective-permute-start.7 = (f32[2,1,4096]{2,1,0:T(1,128)S(1)}, f32[2,1,4096]{2,1,0:T(1,128)S(1)}, u32[]{:S(2)}, u32[]{:S(2)}) collective-permute-start(f32[2,1,4096]{2,1,0:T(1,128)S(1)} %get-tuple-element.360), channel_id=1, source_target_pairs={{1,0},{2,1},{3,2},{4,3},{5,4},{6,5},{7,6},{8,7},{9,8},{10,9},{11,1... | collective-permute-start | bytes 98312 | tf_op jit(solution)/shard_map/ppermute | solution.py:34
  77.3 8.1 %collective-permute-done.6 = f32[2,1,4096]{2,1,0:T(1,128)S(1)} collective-permute-done((f32[2,1,4096]{2,1,0:T(1,128)S(1)}, f32[2,1,4096]{2,1,0:T(1,128)S(1)}, u32[]{:S(2)}, u32[]{:S(2)}) %collective-permute-start.6) | collective-permute-done | bytes 32800 | tf_op jit(solution)/shard_map/ppermute | solution.py:32
  85.9 11.2 %all_to_all.16 = f32[2,8,8,512]{3,2,0,1:T(8,128)S(1)} all-to-all(f32[2,8,8,512]{3,2,0,1:T(8,128)S(1)} %copy.17), channel_id=1, replica_groups=mesh['grp'=2,'row'=8,'col'=8] {'col'}, dimensions={1} | all-to-all | bytes 524288 | tf_op jit(solution)/shard_map/all_to_all | solution.py:192
  102.4 4.3 %collective-permute-done.14 = f32[4,2,4096]{2,1,0:T(2,128)S(1)} collective-permute-done((f32[4,2,4096]{2,1,0:T(2,128)S(1)}, f32[4,2,4096]{2,1,0:T(2,128)S(1)}, u32[]{:S(2)}, u32[]{:S(2)}) %collective-permute-start.14) | collective-permute-done | bytes 131104 | tf_op jit(solution)/shard_map/ppermute | solution.py:34
  106.8 4.3 %collective-permute-done.13 = f32[4,2,4096]{2,1,0:T(2,128)S(1)} collective-permute-done((f32[4,2,4096]{2,1,0:T(2,128)S(1)}, f32[4,2,4096]{2,1,0:T(2,128)S(1)}, u32[]{:S(2)}, u32[]{:S(2)}) %collective-permute-start.13) | collective-permute-done | bytes 131104 | tf_op jit(solution)/shard_map/ppermute | solution.py:32
  115.2 3.5 %collective-permute-start.15 = (f32[2,1,4096]{2,1,0:T(1,128)S(1)}, f32[2,1,4096]{2,1,0:T(1,128)S(1)}, u32[]{:S(2)}, u32[]{:S(2)}) collective-permute-start(f32[2,1,4096]{2,1,0:T(1,128)S(1)} %get-tuple-element.357), channel_id=1, source_target_pairs={{0,1},{1,2},{2,3},{3,4},{4,5},{5,6},{6,7},{7,8},{8,9},{9,10},{10,1... | collective-permute-start | bytes 98312 | tf_op jit(solution)/shard_map/ppermute | solution.py:32
  120.6 4.0 %collective-permute-done.15 = f32[2,1,4096]{2,1,0:T(1,128)S(1)} collective-permute-done((f32[2,1,4096]{2,1,0:T(1,128)S(1)}, f32[2,1,4096]{2,1,0:T(1,128)S(1)}, u32[]{:S(2)}, u32[]{:S(2)}) %collective-permute-start.15) | collective-permute-done | bytes 32800 | tf_op jit(solution)/shard_map/ppermute | solution.py:32
  125.2 3.5 %collective-permute-start.17 = (f32[2,1,4096]{2,1,0:T(1,128)S(1)}, f32[2,1,4096]{2,1,0:T(1,128)S(1)}, u32[]{:S(2)}, u32[]{:S(2)}) collective-permute-start(f32[2,1,4096]{2,1,0:T(1,128)S(1)} %get-tuple-element.355), channel_id=1, source_target_pairs={{0,1},{1,2},{2,3},{3,4},{4,5},{5,6},{6,7},{7,8},{8,9},{9,10},{10,1... | collective-permute-start | bytes 98312 | tf_op jit(solution)/shard_map/ppermute | solution.py:32
  130.6 4.0 %collective-permute-done.17 = f32[2,1,4096]{2,1,0:T(1,128)S(1)} collective-permute-done((f32[2,1,4096]{2,1,0:T(1,128)S(1)}, f32[2,1,4096]{2,1,0:T(1,128)S(1)}, u32[]{:S(2)}, u32[]{:S(2)}) %collective-permute-start.17) | collective-permute-done | bytes 32800 | tf_op jit(solution)/shard_map/ppermute | solution.py:32
  135.3 3.5 %collective-permute-start.19 = (f32[2,1,4096]{2,1,0:T(1,128)S(1)}, f32[2,1,4096]{2,1,0:T(1,128)S(1)}, u32[]{:S(2)}, u32[]{:S(2)}) collective-permute-start(f32[2,1,4096]{2,1,0:T(1,128)S(1)} %get-tuple-element.353), channel_id=1, source_target_pairs={{0,1},{1,2},{2,3},{3,4},{4,5},{5,6},{6,7},{7,8},{8,9},{9,10},{10,1... | collective-permute-start | bytes 98312 | tf_op jit(solution)/shard_map/ppermute | solution.py:32
  140.7 7.0 %collective-permute-done.19 = f32[2,1,4096]{2,1,0:T(1,128)S(1)} collective-permute-done((f32[2,1,4096]{2,1,0:T(1,128)S(1)}, f32[2,1,4096]{2,1,0:T(1,128)S(1)}, u32[]{:S(2)}, u32[]{:S(2)}) %collective-permute-start.19) | collective-permute-done | bytes 32800 | tf_op jit(solution)/shard_map/ppermute | solution.py:32
  149.9 3.5 %all-to-all-start.2 = ((f32[5,8,8,512]{3,2,0,1:T(8,128)}), f32[5,8,8,512]{3,2,0,1:T(8,128)S(1)}, u32[]{:S(2)}, u32[]{:S(2)}) async-start(f32[5,8,8,512]{3,2,0,1:T(8,128)} %copy.20), calls=%async_computation.2 | async-start | bytes 1310720 | tf_op jit(solution)/shard_map/all_to_all | solution.py:192
  160.1 5.6 %collective-permute-start.24 = (f32[7,68,2]{2,1,0:T(8,128)S(1)}, f32[7,68,2]{2,1,0:T(8,128)S(1)}, u32[]{:S(2)}, u32[]{:S(2)}) collective-permute-start(f32[7,68,2]{2,1,0:T(8,128)S(1)} %get-tuple-element.324), channel_id=1, source_target_pairs={{1,0},{2,1},{3,2},{4,3},{5,4},{6,5},{7,6},{0,7},{9,8},{10,9},{11,1... | collective-permute-start | bytes 11432 | tf_op jit(solution)/shard_map/ppermute | solution.py:34
  165.7 4.3 %collective-permute-done.24 = f32[7,68,2]{2,1,0:T(8,128)S(1)} collective-permute-done((f32[7,68,2]{2,1,0:T(8,128)S(1)}, f32[7,68,2]{2,1,0:T(8,128)S(1)}, u32[]{:S(2)}, u32[]{:S(2)}) %collective-permute-start.24) | collective-permute-done | bytes 3840 | tf_op jit(solution)/shard_map/ppermute | solution.py:34
  170.0 8.4 %collective-permute-done.23 = f32[7,68,2]{2,1,0:T(8,128)S(1)} collective-permute-done((f32[7,68,2]{2,1,0:T(8,128)S(1)}, f32[7,68,2]{2,1,0:T(8,128)S(1)}, u32[]{:S(2)}, u32[]{:S(2)}) %collective-permute-start.23) | collective-permute-done | bytes 3840 | tf_op jit(solution)/shard_map/ppermute | solution.py:32
  179.0 6.9 %conditional.23 = (f32[5,64,512]{2,1,0:T(8,128)S(1)}) conditional(s32[]{:T(128)} %convert_element_type.2, (f32[7,68,516]{2,1,0:T(8,128)S(1)}, f32[5,64,512]{2,1,0:T(8,128)S(1)}) %tuple.90, f32[5,64,512]{2,1,0:T(8,128)S(1)} %get-tuple-element.376), branch_computations={%region_22.23_spmd, %region_23.24_spmd} | conditional | flops 12940432 | bytes 60802312 | solution.py:218
  (200 shorter events, 59.0 us)
Async XLA Ops:
  18.8 7.7 %collective-permute-start.1 = (f32[4,2,4096]{2,1,0:T(2,128)S(1)}, f32[4,2,4096]{2,1,0:T(2,128)S(1)}, u32[]{:S(2)}, u32[]{:S(2)}) collective-permute-start(f32[4,2,4096]{2,1,0:T(2,128)S(1)} %get-tuple-element.352), channel_id=1, source_target_pairs={{1,0},{2,1},{3,2},{4,3},{5,4},{6,5},{7,6},{8,7},{9,8},{10,9},{11,1... | collective-permute-start | bytes 393224 | tf_op jit(solution)/shard_map/ppermute | solution.py:34
  22.5 10.7 %collective-permute-start = (f32[4,2,4096]{2,1,0:T(2,128)S(1)}, f32[4,2,4096]{2,1,0:T(2,128)S(1)}, u32[]{:S(2)}, u32[]{:S(2)}) collective-permute-start(f32[4,2,4096]{2,1,0:T(2,128)S(1)} %get-tuple-element.351), channel_id=1, source_target_pairs={{0,1},{1,2},{2,3},{3,4},{4,5},{5,6},{6,7},{7,8},{8,9},{9,10},{10,1... | collective-permute-start | bytes 393224 | tf_op jit(solution)/shard_map/ppermute | solution.py:32
  22.6 17.1 %collective-permute-start.9 = (f32[7,2,512]{2,1,0:T(2,128)S(1)}, f32[7,2,512]{2,1,0:T(2,128)S(1)}, u32[]{:S(2)}, u32[]{:S(2)}) collective-permute-start(f32[7,2,512]{2,1,0:T(2,128)S(1)} %get-tuple-element.330), channel_id=1, source_target_pairs={{8,0},{16,8},{24,16},{32,24},{40,32},{48,40},{56,48},{0,56},{9,1},... | collective-permute-start | bytes 86024 | tf_op jit(solution)/shard_map/ppermute | solution.py:34
  25.6 14.2 %collective-permute-start.8 = (f32[7,2,512]{2,1,0:T(2,128)S(1)}, f32[7,2,512]{2,1,0:T(2,128)S(1)}, u32[]{:S(2)}, u32[]{:S(2)}) collective-permute-start(f32[7,2,512]{2,1,0:T(2,128)S(1)} %get-tuple-element.329), channel_id=1, source_target_pairs={{0,8},{8,16},{16,24},{24,32},{32,40},{40,48},{48,56},{56,0},{1,9},... | collective-permute-start | bytes 86024 | tf_op jit(solution)/shard_map/ppermute | solution.py:32
  36.1 14.6 %collective-permute-start.3 = (f32[2,1,4096]{2,1,0:T(1,128)S(1)}, f32[2,1,4096]{2,1,0:T(1,128)S(1)}, u32[]{:S(2)}, u32[]{:S(2)}) collective-permute-start(f32[2,1,4096]{2,1,0:T(1,128)S(1)} %get-tuple-element.364), channel_id=1, source_target_pairs={{1,0},{2,1},{3,2},{4,3},{5,4},{6,5},{7,6},{8,7},{9,8},{10,9},{11,1... | collective-permute-start | bytes 98312 | tf_op jit(solution)/shard_map/ppermute | solution.py:34
  37.4 17.0 %collective-permute-start.2 = (f32[2,1,4096]{2,1,0:T(1,128)S(1)}, f32[2,1,4096]{2,1,0:T(1,128)S(1)}, u32[]{:S(2)}, u32[]{:S(2)}) collective-permute-start(f32[2,1,4096]{2,1,0:T(1,128)S(1)} %get-tuple-element.363), channel_id=1, source_target_pairs={{0,1},{1,2},{2,3},{3,4},{4,5},{5,6},{6,7},{7,8},{8,9},{9,10},{10,1... | collective-permute-start | bytes 98312 | tf_op jit(solution)/shard_map/ppermute | solution.py:32
  39.9 19.3 %collective-permute-start.11 = (f32[7,68,2]{2,1,0:T(8,128)S(1)}, f32[7,68,2]{2,1,0:T(8,128)}, u32[]{:S(2)}, u32[]{:S(2)}) collective-permute-start(f32[7,68,2]{2,1,0:T(8,128)S(1)} %get-tuple-element.326), channel_id=1, source_target_pairs={{1,0},{2,1},{3,2},{4,3},{5,4},{6,5},{7,6},{0,7},{9,8},{10,9},{11,1... | collective-permute-start | bytes 11432 | tf_op jit(solution)/shard_map/ppermute | solution.py:34
  41.3 17.9 %collective-permute-start.10 = (f32[7,68,2]{2,1,0:T(8,128)S(1)}, f32[7,68,2]{2,1,0:T(8,128)}, u32[]{:S(2)}, u32[]{:S(2)}) collective-permute-start(f32[7,68,2]{2,1,0:T(8,128)S(1)} %get-tuple-element.325), channel_id=1, source_target_pairs={{0,1},{1,2},{2,3},{3,4},{4,5},{5,6},{6,7},{7,0},{8,9},{9,10},{10,1... | collective-permute-start | bytes 11432 | tf_op jit(solution)/shard_map/ppermute | solution.py:32
  54.9 12.7 %collective-permute-start.5 = (f32[2,1,4096]{2,1,0:T(1,128)S(1)}, f32[2,1,4096]{2,1,0:T(1,128)S(1)}, u32[]{:S(2)}, u32[]{:S(2)}) collective-permute-start(f32[2,1,4096]{2,1,0:T(1,128)S(1)} %get-tuple-element.362), channel_id=1, source_target_pairs={{1,0},{2,1},{3,2},{4,3},{5,4},{6,5},{7,6},{8,7},{9,8},{10,9},{11,1... | collective-permute-start | bytes 98312 | tf_op jit(solution)/shard_map/ppermute | solution.py:34
  59.2 9.3 %collective-permute-start.4 = (f32[2,1,4096]{2,1,0:T(1,128)S(1)}, f32[2,1,4096]{2,1,0:T(1,128)S(1)}, u32[]{:S(2)}, u32[]{:S(2)}) collective-permute-start(f32[2,1,4096]{2,1,0:T(1,128)S(1)} %get-tuple-element.361), channel_id=1, source_target_pairs={{0,1},{1,2},{2,3},{3,4},{4,5},{5,6},{6,7},{7,8},{8,9},{9,10},{10,1... | collective-permute-start | bytes 98312 | tf_op jit(solution)/shard_map/ppermute | solution.py:32
  69.0 8.3 %collective-permute-start.7 = (f32[2,1,4096]{2,1,0:T(1,128)S(1)}, f32[2,1,4096]{2,1,0:T(1,128)S(1)}, u32[]{:S(2)}, u32[]{:S(2)}) collective-permute-start(f32[2,1,4096]{2,1,0:T(1,128)S(1)} %get-tuple-element.360), channel_id=1, source_target_pairs={{1,0},{2,1},{3,2},{4,3},{5,4},{6,5},{7,6},{8,7},{9,8},{10,9},{11,1... | collective-permute-start | bytes 98312 | tf_op jit(solution)/shard_map/ppermute | solution.py:34
  75.7 9.7 %collective-permute-start.6 = (f32[2,1,4096]{2,1,0:T(1,128)S(1)}, f32[2,1,4096]{2,1,0:T(1,128)S(1)}, u32[]{:S(2)}, u32[]{:S(2)}) collective-permute-start(f32[2,1,4096]{2,1,0:T(1,128)S(1)} %get-tuple-element.359), channel_id=1, source_target_pairs={{0,1},{1,2},{2,3},{3,4},{4,5},{5,6},{6,7},{7,8},{8,9},{9,10},{10,1... | collective-permute-start | bytes 98312 | tf_op jit(solution)/shard_map/ppermute | solution.py:32
  98.8 7.9 %collective-permute-start.14 = (f32[4,2,4096]{2,1,0:T(2,128)S(1)}, f32[4,2,4096]{2,1,0:T(2,128)S(1)}, u32[]{:S(2)}, u32[]{:S(2)}) collective-permute-start(f32[4,2,4096]{2,1,0:T(2,128)S(1)} %get-tuple-element.344), channel_id=1, source_target_pairs={{1,0},{2,1},{3,2},{4,3},{5,4},{6,5},{7,6},{8,7},{9,8},{10,9},{11,1... | collective-permute-start | bytes 393224 | tf_op jit(solution)/shard_map/ppermute | solution.py:34
  100.1 11.0 %collective-permute-start.13 = (f32[4,2,4096]{2,1,0:T(2,128)S(1)}, f32[4,2,4096]{2,1,0:T(2,128)S(1)}, u32[]{:S(2)}, u32[]{:S(2)}) collective-permute-start(f32[4,2,4096]{2,1,0:T(2,128)S(1)} %get-tuple-element.343), channel_id=1, source_target_pairs={{0,1},{1,2},{2,3},{3,4},{4,5},{5,6},{6,7},{7,8},{8,9},{9,10},{10,1... | collective-permute-start | bytes 393224 | tf_op jit(solution)/shard_map/ppermute | solution.py:32
  115.1 5.5 %collective-permute-start.16 = (f32[2,1,4096]{2,1,0:T(1,128)S(1)}, f32[2,1,4096]{2,1,0:T(1,128)S(1)}, u32[]{:S(2)}, u32[]{:S(2)}) collective-permute-start(f32[2,1,4096]{2,1,0:T(1,128)S(1)} %get-tuple-element.358), channel_id=1, source_target_pairs={{1,0},{2,1},{3,2},{4,3},{5,4},{6,5},{7,6},{8,7},{9,8},{10,9},{11,1... | collective-permute-start | bytes 98312 | tf_op jit(solution)/shard_map/ppermute | solution.py:34
  115.2 9.4 %collective-permute-start.15 = (f32[2,1,4096]{2,1,0:T(1,128)S(1)}, f32[2,1,4096]{2,1,0:T(1,128)S(1)}, u32[]{:S(2)}, u32[]{:S(2)}) collective-permute-start(f32[2,1,4096]{2,1,0:T(1,128)S(1)} %get-tuple-element.357), channel_id=1, source_target_pairs={{0,1},{1,2},{2,3},{3,4},{4,5},{5,6},{6,7},{7,8},{8,9},{9,10},{10,1... | collective-permute-start | bytes 98312 | tf_op jit(solution)/shard_map/ppermute | solution.py:32
  125.1 5.5 %collective-permute-start.18 = (f32[2,1,4096]{2,1,0:T(1,128)S(1)}, f32[2,1,4096]{2,1,0:T(1,128)S(1)}, u32[]{:S(2)}, u32[]{:S(2)}) collective-permute-start(f32[2,1,4096]{2,1,0:T(1,128)S(1)} %get-tuple-element.356), channel_id=1, source_target_pairs={{1,0},{2,1},{3,2},{4,3},{5,4},{6,5},{7,6},{8,7},{9,8},{10,9},{11,1... | collective-permute-start | bytes 98312 | tf_op jit(solution)/shard_map/ppermute | solution.py:34
  125.2 9.4 %collective-permute-start.17 = (f32[2,1,4096]{2,1,0:T(1,128)S(1)}, f32[2,1,4096]{2,1,0:T(1,128)S(1)}, u32[]{:S(2)}, u32[]{:S(2)}) collective-permute-start(f32[2,1,4096]{2,1,0:T(1,128)S(1)} %get-tuple-element.355), channel_id=1, source_target_pairs={{0,1},{1,2},{2,3},{3,4},{4,5},{5,6},{6,7},{7,8},{8,9},{9,10},{10,1... | collective-permute-start | bytes 98312 | tf_op jit(solution)/shard_map/ppermute | solution.py:32
  135.2 5.5 %collective-permute-start.20 = (f32[2,1,4096]{2,1,0:T(1,128)S(1)}, f32[2,1,4096]{2,1,0:T(1,128)S(1)}, u32[]{:S(2)}, u32[]{:S(2)}) collective-permute-start(f32[2,1,4096]{2,1,0:T(1,128)S(1)} %get-tuple-element.354), channel_id=1, source_target_pairs={{1,0},{2,1},{3,2},{4,3},{5,4},{6,5},{7,6},{8,7},{9,8},{10,9},{11,1... | collective-permute-start | bytes 98312 | tf_op jit(solution)/shard_map/ppermute | solution.py:34
  135.3 12.5 %collective-permute-start.19 = (f32[2,1,4096]{2,1,0:T(1,128)S(1)}, f32[2,1,4096]{2,1,0:T(1,128)S(1)}, u32[]{:S(2)}, u32[]{:S(2)}) collective-permute-start(f32[2,1,4096]{2,1,0:T(1,128)S(1)} %get-tuple-element.353), channel_id=1, source_target_pairs={{0,1},{1,2},{2,3},{3,4},{4,5},{5,6},{6,7},{7,8},{8,9},{9,10},{10,1... | collective-permute-start | bytes 98312 | tf_op jit(solution)/shard_map/ppermute | solution.py:32
  149.9 36.0 %all-to-all-start.2 = ((f32[5,8,8,512]{3,2,0,1:T(8,128)}), f32[5,8,8,512]{3,2,0,1:T(8,128)S(1)}, u32[]{:S(2)}, u32[]{:S(2)}) async-start(f32[5,8,8,512]{3,2,0,1:T(8,128)} %copy.20), calls=%async_computation.2 | async-start | bytes 1310720 | tf_op jit(solution)/shard_map/all_to_all | solution.py:192
  153.6 6.4 %collective-permute-start.21 = (f32[7,2,512]{2,1,0:T(2,128)S(1)}, f32[7,2,512]{2,1,0:T(2,128)S(1)}, u32[]{:S(2)}, u32[]{:S(2)}) collective-permute-start(f32[7,2,512]{2,1,0:T(2,128)S(1)} %get-tuple-element.327), channel_id=1, source_target_pairs={{0,8},{8,16},{16,24},{24,32},{32,40},{40,48},{48,56},{56,0},{1,9},... | collective-permute-start | bytes 86024 | tf_op jit(solution)/shard_map/ppermute | solution.py:32
  160.1 9.9 %collective-permute-start.24 = (f32[7,68,2]{2,1,0:T(8,128)S(1)}, f32[7,68,2]{2,1,0:T(8,128)S(1)}, u32[]{:S(2)}, u32[]{:S(2)}) collective-permute-start(f32[7,68,2]{2,1,0:T(8,128)S(1)} %get-tuple-element.324), channel_id=1, source_target_pairs={{1,0},{2,1},{3,2},{4,3},{5,4},{6,5},{7,6},{0,7},{9,8},{10,9},{11,1... | collective-permute-start | bytes 11432 | tf_op jit(solution)/shard_map/ppermute | solution.py:34
  165.7 12.7 %collective-permute-start.23 = (f32[7,68,2]{2,1,0:T(8,128)S(1)}, f32[7,68,2]{2,1,0:T(8,128)S(1)}, u32[]{:S(2)}, u32[]{:S(2)}) collective-permute-start(f32[7,68,2]{2,1,0:T(8,128)S(1)} %get-tuple-element.323), channel_id=1, source_target_pairs={{0,1},{1,2},{2,3},{3,4},{4,5},{5,6},{6,7},{7,0},{8,9},{9,10},{10,1... | collective-permute-start | bytes 11432 | tf_op jit(solution)/shard_map/ppermute | solution.py:32
  (5 other events, 12.5 us)
where the time goes:
time: 187 us
  waiting for transfers between devices  77.1 us (41%)
  starting transfers between devices  50.6 us (27%)
  blocking collectives  27.7 us (15%)
  other arithmetic  18.6 us (10%)
  local copies, waits for them, and re-layouts  11.2 us (6%)
    ppermute x12, waiting for transfers between devices, with_halo(): lax.ppermute(tail, axis, [(i, (i + 1) % count) for i in range(count)])  48.6 us
    all_to_all x2, blocking collectives, regroup(): lax.all_to_all(values, 'col', split_axis=1, concat_axis=1, tiled=True)  27.7 us
    ppermute x12, starting transfers between devices, with_halo(): lax.ppermute(head, axis, [((i + 1) % count, i) for i in range(count)])  27.6 us
    ppermute x12, waiting for transfers between devices, with_halo(): lax.ppermute(head, axis, [((i + 1) % count, i) for i in range(count)])  26.9 us
    ppermute x12, starting transfers between devices, with_halo(): lax.ppermute(tail, axis, [(i, (i + 1) % count) for i in range(count)])  19.4 us
    concatenate x8, local copies, waits for them, and re-layouts, slab_extend(): jnp.concatenate([extended[:, :, -margin:], extended, extended[:, :, :marg...  5.05 us
  transfers between devices with their start and end apart: 26, of which 20 were waited for; matrix products, arithmetic and copies ran while one was open for 10% of the time, Pallas kernels for 0%

commit v1 on v0

--- a/solution.py
+++ b/solution.py
@@ -10,6 +10,15 @@
 GRADIENT_GAIN = 8.0
 MONITOR_GAIN = 0.2
 RELAXATION = 0.5
+
+
+def play_the_vectors(q_in, row_dim, array_axis):
+    local_part = lax.psum(1, "col")
+    earlier = jnp.split(q_in, local_part, axis=row_dim)
+    taken_in = jnp.stack(earlier, axis=0)
+    inter = lax.all_to_all(taken_in, "col", 0, 0)
+    x_next = jnp.concatenate(inter, axis=array_axis)
+    return x_next
 
 
 def partner(block, axis, apart):
@@ -189,7 +198,7 @@
         )
 
     def regroup(values):
-        return lax.all_to_all(values, "col", split_axis=1, concat_axis=1, tiled=True)
+        return play_the_vectors(values, 1, 1)
 
     def only_mesh(worker, fallback, operands):
         return lax.cond(on_mesh, lambda packed: worker(*packed), lambda packed: fallback, operands)

time: 187 us -> 193 us (1.032)
  blocking collectives: 27.7 us -> 11.2 us
  waiting for transfers between devices: 77.1 us -> 86.4 us
  starting transfers between devices: 50.6 us -> 58.5 us
  local copies, waits for them, and re-layouts: 11.2 us -> 16.5 us
    all_to_all x2 -> x1, blocking collectives: 27.7 us -> 11.2 us  [play_the_vectors(): inter = lax.all_to_all(taken_in, 'col', 0, 0)]
    all_to_all x1 -> x2, waiting for transfers between devices: 0.01 us -> 8.79 us  [play_the_vectors(): inter = lax.all_to_all(taken_in, 'col', 0, 0)]
    all_to_all x1 -> x2, starting transfers between devices: 3.54 us -> 11.4 us  [play_the_vectors(): inter = lax.all_to_all(taken_in, 'col', 0, 0)]
    unnamed x9 -> x30, local copies, waits for them, and re-layouts: 2.94 us -> 7.88 us
  transfers between devices with their start and end apart: 26 -> 27, of which waited for: 20 -> 21; matrix products, arithmetic and copies ran while one was open for 10% -> 9% of each run, Pallas kernels for 0% -> 0%
where the time goes in v1:
time: 193 us
  waiting for transfers between devices  86.4 us (45%)
  starting transfers between devices  58.5 us (30%)
  other arithmetic  18.6 us (10%)
  local copies, waits for them, and re-layouts  16.5 us (9%)
  blocking collectives  11.2 us (6%)
    ppermute x12, waiting for transfers between devices, with_halo(): lax.ppermute(tail, axis, [(i, (i + 1) % count) for i in range(count)])  49 us
    ppermute x12, starting transfers between devices, with_halo(): lax.ppermute(head, axis, [((i + 1) % count, i) for i in range(count)])  27.5 us
    ppermute x12, waiting for transfers between devices, with_halo(): lax.ppermute(head, axis, [((i + 1) % count, i) for i in range(count)])  27 us
    ppermute x12, starting transfers between devices, with_halo(): lax.ppermute(tail, axis, [(i, (i + 1) % count) for i in range(count)])  19.4 us
    all_to_all x2, starting transfers between devices, play_the_vectors(): inter = lax.all_to_all(taken_in, 'col', 0, 0)  11.4 us
    all_to_all x1, blocking collectives, play_the_vectors(): inter = lax.all_to_all(taken_in, 'col', 0, 0)  11.2 us
    all_to_all x2, waiting for transfers between devices, play_the_vectors(): inter = lax.all_to_all(taken_in, 'col', 0, 0)  8.79 us
    unnamed x30, local copies, waits for them, and re-layouts  7.88 us
  transfers between devices with their start and end apart: 27, of which 21 were waited for; matrix products, arithmetic and copies ran while one was open for 9% of the time, Pallas kernels for 0%

profile of v1, /device:TPU:0, one launch (start us, length us, event | category | flops | bytes accessed | tf_op | source)
XLA Modules:
  0.0 193.0 jit_solution(1690122038663552899)
XLA Ops:
  7.1 7.9 %all-to-all-start = ((f32[8,2,1,8,512]{4,3,1,2,0:T(8,128)}), f32[8,2,1,8,512]{4,3,1,2,0:T(8,128)S(1)}, u32[]{:S(2)}, u32[]{:S(2)}) async-start(f32[8,2,1,8,512]{4,3,1,2,0:T(8,128)} %constant_dynamic-update-slice_fusion.12), calls=%async_computation | async-start | bytes 524288 | tf_op jit(solution)/shard_map/all_to_all | solution.py:19
  15.0 8.8 %all-to-all-done = f32[8,2,1,8,512]{4,3,1,2,0:T(8,128)S(1)} async-done(((f32[8,2,1,8,512]{4,3,1,2,0:T(8,128)}), f32[8,2,1,8,512]{4,3,1,2,0:T(8,128)S(1)}, u32[]{:S(2)}, u32[]{:S(2)}) %all-to-all-start) | async-done | bytes 262176 | tf_op jit(solution)/shard_map/all_to_all | solution.py:19
  23.9 3.7 %collective-permute-start.1 = (f32[4,2,4096]{2,1,0:T(2,128)S(1)}, f32[4,2,4096]{2,1,0:T(2,128)S(1)}, u32[]{:S(2)}, u32[]{:S(2)}) collective-permute-start(f32[4,2,4096]{2,1,0:T(2,128)S(1)} %get-tuple-element.352), channel_id=1, source_target_pairs={{1,0},{2,1},{3,2},{4,3},{5,4},{6,5},{7,6},{8,7},{9,8},{10,9},{11,1... | collective-permute-start | bytes 393224 | tf_op jit(solution)/shard_map/ppermute | solution.py:43
  31.6 6.7 %collective-permute-done = f32[4,2,4096]{2,1,0:T(2,128)S(1)} collective-permute-done((f32[4,2,4096]{2,1,0:T(2,128)S(1)}, f32[4,2,4096]{2,1,0:T(2,128)S(1)}, u32[]{:S(2)}, u32[]{:S(2)}) %collective-permute-start) | collective-permute-done | bytes 131104 | tf_op jit(solution)/shard_map/ppermute | solution.py:41
  48.6 7.2 %collective-permute-done.3 = f32[2,1,4096]{2,1,0:T(1,128)S(1)} collective-permute-done((f32[2,1,4096]{2,1,0:T(1,128)S(1)}, f32[2,1,4096]{2,1,0:T(1,128)S(1)}, u32[]{:S(2)}, u32[]{:S(2)}) %collective-permute-start.3) | collective-permute-done | bytes 32800 | tf_op jit(solution)/shard_map/ppermute | solution.py:43
  55.8 3.7 %collective-permute-done.2 = f32[2,1,4096]{2,1,0:T(1,128)S(1)} collective-permute-done((f32[2,1,4096]{2,1,0:T(1,128)S(1)}, f32[2,1,4096]{2,1,0:T(1,128)S(1)}, u32[]{:S(2)}, u32[]{:S(2)}) %collective-permute-start.2) | collective-permute-done | bytes 32800 | tf_op jit(solution)/shard_map/ppermute | solution.py:41
  60.0 4.3 %collective-permute-start.5 = (f32[2,1,4096]{2,1,0:T(1,128)S(1)}, f32[2,1,4096]{2,1,0:T(1,128)S(1)}, u32[]{:S(2)}, u32[]{:S(2)}) collective-permute-start(f32[2,1,4096]{2,1,0:T(1,128)S(1)} %get-tuple-element.362), channel_id=1, source_target_pairs={{1,0},{2,1},{3,2},{4,3},{5,4},{6,5},{7,6},{8,7},{9,8},{10,9},{11,1... | collective-permute-start | bytes 98312 | tf_op jit(solution)/shard_map/ppermute | solution.py:43
  66.0 6.8 %conditional.17 = (f32[5,64,512]{2,1,0:T(8,128)S(1)}) conditional(s32[]{:T(128)} %convert_element_type.2, (f32[7,68,516]{2,1,0:T(8,128)S(1)}, f32[5,64,512]{2,1,0:T(8,128)S(1)}) %tuple.239, f32[5,64,512]{2,1,0:T(8,128)S(1)} %copy-done), branch_computations={%region_10.11_spmd, %region_11.12_spmd} | conditional | flops 12940432 | bytes 60802312 | solution.py:227
  74.1 6.7 %collective-permute-start.7 = (f32[2,1,4096]{2,1,0:T(1,128)S(1)}, f32[2,1,4096]{2,1,0:T(1,128)S(1)}, u32[]{:S(2)}, u32[]{:S(2)}) collective-permute-start(f32[2,1,4096]{2,1,0:T(1,128)S(1)} %get-tuple-element.360), channel_id=1, source_target_pairs={{1,0},{2,1},{3,2},{4,3},{5,4},{6,5},{7,6},{8,7},{9,8},{10,9},{11,1... | collective-permute-start | bytes 98312 | tf_op jit(solution)/shard_map/ppermute | solution.py:43
  82.4 8.2 %collective-permute-done.6 = f32[2,1,4096]{2,1,0:T(1,128)S(1)} collective-permute-done((f32[2,1,4096]{2,1,0:T(1,128)S(1)}, f32[2,1,4096]{2,1,0:T(1,128)S(1)}, u32[]{:S(2)}, u32[]{:S(2)}) %collective-permute-start.6) | collective-permute-done | bytes 32800 | tf_op jit(solution)/shard_map/ppermute | solution.py:41
  91.2 11.2 %all_to_all.15 = f32[8,2,1,8,512]{4,3,1,2,0:T(8,128)S(1)} all-to-all(f32[8,2,1,8,512]{4,3,1,2,0:T(8,128)S(1)} %constant_dynamic-update-slice_fusion.22), channel_id=1, replica_groups=mesh['grp'=2,'row'=8,'col'=8] {'col'}, dimensions={0} | all-to-all | bytes 524288 | tf_op jit(solution)/shard_map/all_to_all | solution.py:19
  107.7 4.3 %collective-permute-done.14 = f32[4,2,4096]{2,1,0:T(2,128)S(1)} collective-permute-done((f32[4,2,4096]{2,1,0:T(2,128)S(1)}, f32[4,2,4096]{2,1,0:T(2,128)S(1)}, u32[]{:S(2)}, u32[]{:S(2)}) %collective-permute-start.14) | collective-permute-done | bytes 131104 | tf_op jit(solution)/shard_map/ppermute | solution.py:43
  112.0 4.3 %collective-permute-done.13 = f32[4,2,4096]{2,1,0:T(2,128)S(1)} collective-permute-done((f32[4,2,4096]{2,1,0:T(2,128)S(1)}, f32[4,2,4096]{2,1,0:T(2,128)S(1)}, u32[]{:S(2)}, u32[]{:S(2)}) %collective-permute-start.13) | collective-permute-done | bytes 131104 | tf_op jit(solution)/shard_map/ppermute | solution.py:41
  120.4 3.5 %collective-permute-start.15 = (f32[2,1,4096]{2,1,0:T(1,128)S(1)}, f32[2,1,4096]{2,1,0:T(1,128)S(1)}, u32[]{:S(2)}, u32[]{:S(2)}) collective-permute-start(f32[2,1,4096]{2,1,0:T(1,128)S(1)} %get-tuple-element.357), channel_id=1, source_target_pairs={{0,1},{1,2},{2,3},{3,4},{4,5},{5,6},{6,7},{7,8},{8,9},{9,10},{10,1... | collective-permute-start | bytes 98312 | tf_op jit(solution)/shard_map/ppermute | solution.py:41
  125.8 4.0 %collective-permute-done.15 = f32[2,1,4096]{2,1,0:T(1,128)S(1)} collective-permute-done((f32[2,1,4096]{2,1,0:T(1,128)S(1)}, f32[2,1,4096]{2,1,0:T(1,128)S(1)}, u32[]{:S(2)}, u32[]{:S(2)}) %collective-permute-start.15) | collective-permute-done | bytes 32800 | tf_op jit(solution)/shard_map/ppermute | solution.py:41
  130.4 3.5 %collective-permute-start.17 = (f32[2,1,4096]{2,1,0:T(1,128)S(1)}, f32[2,1,4096]{2,1,0:T(1,128)S(1)}, u32[]{:S(2)}, u32[]{:S(2)}) collective-permute-start(f32[2,1,4096]{2,1,0:T(1,128)S(1)} %get-tuple-element.355), channel_id=1, source_target_pairs={{0,1},{1,2},{2,3},{3,4},{4,5},{5,6},{6,7},{7,8},{8,9},{9,10},{10,1... | collective-permute-start | bytes 98312 | tf_op jit(solution)/shard_map/ppermute | solution.py:41
  135.8 4.0 %collective-permute-done.17 = f32[2,1,4096]{2,1,0:T(1,128)S(1)} collective-permute-done((f32[2,1,4096]{2,1,0:T(1,128)S(1)}, f32[2,1,4096]{2,1,0:T(1,128)S(1)}, u32[]{:S(2)}, u32[]{:S(2)}) %collective-permute-start.17) | collective-permute-done | bytes 32800 | tf_op jit(solution)/shard_map/ppermute | solution.py:41
  140.5 3.5 %collective-permute-start.19 = (f32[2,1,4096]{2,1,0:T(1,128)S(1)}, f32[2,1,4096]{2,1,0:T(1,128)S(1)}, u32[]{:S(2)}, u32[]{:S(2)}) collective-permute-start(f32[2,1,4096]{2,1,0:T(1,128)S(1)} %get-tuple-element.353), channel_id=1, source_target_pairs={{0,1},{1,2},{2,3},{3,4},{4,5},{5,6},{6,7},{7,8},{8,9},{9,10},{10,1... | collective-permute-start | bytes 98312 | tf_op jit(solution)/shard_map/ppermute | solution.py:41
  145.9 7.6 %collective-permute-done.19 = f32[2,1,4096]{2,1,0:T(1,128)S(1)} collective-permute-done((f32[2,1,4096]{2,1,0:T(1,128)S(1)}, f32[2,1,4096]{2,1,0:T(1,128)S(1)}, u32[]{:S(2)}, u32[]{:S(2)}) %collective-permute-start.19) | collective-permute-done | bytes 32800 | tf_op jit(solution)/shard_map/ppermute | solution.py:41
  156.0 3.5 %all-to-all-start.2 = ((f32[8,5,1,8,512]{4,3,1,2,0:T(8,128)}), f32[8,5,1,8,512]{4,3,1,2,0:T(8,128)S(1)}, u32[]{:S(2)}, u32[]{:S(2)}) async-start(f32[8,5,1,8,512]{4,3,1,2,0:T(8,128)} %copy.57), calls=%async_computation.2 | async-start | bytes 1310720 | tf_op jit(solution)/shard_map/all_to_all | solution.py:19
  166.2 5.6 %collective-permute-start.24 = (f32[7,68,2]{2,1,0:T(8,128)S(1)}, f32[7,68,2]{2,1,0:T(8,128)S(1)}, u32[]{:S(2)}, u32[]{:S(2)}) collective-permute-start(f32[7,68,2]{2,1,0:T(8,128)S(1)} %get-tuple-element.324), channel_id=1, source_target_pairs={{1,0},{2,1},{3,2},{4,3},{5,4},{6,5},{7,6},{0,7},{9,8},{10,9},{11,1... | collective-permute-start | bytes 11432 | tf_op jit(solution)/shard_map/ppermute | solution.py:43
  171.8 4.4 %collective-permute-done.24 = f32[7,68,2]{2,1,0:T(8,128)S(1)} collective-permute-done((f32[7,68,2]{2,1,0:T(8,128)S(1)}, f32[7,68,2]{2,1,0:T(8,128)S(1)}, u32[]{:S(2)}, u32[]{:S(2)}) %collective-permute-start.24) | collective-permute-done | bytes 3840 | tf_op jit(solution)/shard_map/ppermute | solution.py:43
  176.2 8.3 %collective-permute-done.23 = f32[7,68,2]{2,1,0:T(8,128)S(1)} collective-permute-done((f32[7,68,2]{2,1,0:T(8,128)S(1)}, f32[7,68,2]{2,1,0:T(8,128)S(1)}, u32[]{:S(2)}, u32[]{:S(2)}) %collective-permute-start.23) | collective-permute-done | bytes 3840 | tf_op jit(solution)/shard_map/ppermute | solution.py:41
  185.1 6.9 %conditional.23 = (f32[5,64,512]{2,1,0:T(8,128)S(1)}) conditional(s32[]{:T(128)} %convert_element_type.2, (f32[7,68,516]{2,1,0:T(8,128)S(1)}, f32[5,64,512]{2,1,0:T(8,128)S(1)}) %tuple.90, f32[5,64,512]{2,1,0:T(8,128)S(1)} %get-tuple-element.376), branch_computations={%region_22.23_spmd, %region_23.24_spmd} | conditional | flops 12940432 | bytes 60802312 | solution.py:227
  (223 shorter events, 67.2 us)
Async XLA Ops:
  7.1 16.7 %all-to-all-start = ((f32[8,2,1,8,512]{4,3,1,2,0:T(8,128)}), f32[8,2,1,8,512]{4,3,1,2,0:T(8,128)S(1)}, u32[]{:S(2)}, u32[]{:S(2)}) async-start(f32[8,2,1,8,512]{4,3,1,2,0:T(8,128)} %constant_dynamic-update-slice_fusion.12), calls=%async_computation | async-start | bytes 524288 | tf_op jit(solution)/shard_map/all_to_all | solution.py:19
  23.9 7.7 %collective-permute-start.1 = (f32[4,2,4096]{2,1,0:T(2,128)S(1)}, f32[4,2,4096]{2,1,0:T(2,128)S(1)}, u32[]{:S(2)}, u32[]{:S(2)}) collective-permute-start(f32[4,2,4096]{2,1,0:T(2,128)S(1)} %get-tuple-element.352), channel_id=1, source_target_pairs={{1,0},{2,1},{3,2},{4,3},{5,4},{6,5},{7,6},{8,7},{9,8},{10,9},{11,1... | collective-permute-start | bytes 393224 | tf_op jit(solution)/shard_map/ppermute | solution.py:43
  27.6 10.7 %collective-permute-start = (f32[4,2,4096]{2,1,0:T(2,128)S(1)}, f32[4,2,4096]{2,1,0:T(2,128)S(1)}, u32[]{:S(2)}, u32[]{:S(2)}) collective-permute-start(f32[4,2,4096]{2,1,0:T(2,128)S(1)} %get-tuple-element.351), channel_id=1, source_target_pairs={{0,1},{1,2},{2,3},{3,4},{4,5},{5,6},{6,7},{7,8},{8,9},{9,10},{10,1... | collective-permute-start | bytes 393224 | tf_op jit(solution)/shard_map/ppermute | solution.py:41
  27.7 17.1 %collective-permute-start.9 = (f32[7,2,512]{2,1,0:T(2,128)S(1)}, f32[7,2,512]{2,1,0:T(2,128)S(1)}, u32[]{:S(2)}, u32[]{:S(2)}) collective-permute-start(f32[7,2,512]{2,1,0:T(2,128)S(1)} %get-tuple-element.330), channel_id=1, source_target_pairs={{8,0},{16,8},{24,16},{32,24},{40,32},{48,40},{56,48},{0,56},{9,1},... | collective-permute-start | bytes 86024 | tf_op jit(solution)/shard_map/ppermute | solution.py:43
  30.7 14.1 %collective-permute-start.8 = (f32[7,2,512]{2,1,0:T(2,128)S(1)}, f32[7,2,512]{2,1,0:T(2,128)S(1)}, u32[]{:S(2)}, u32[]{:S(2)}) collective-permute-start(f32[7,2,512]{2,1,0:T(2,128)S(1)} %get-tuple-element.329), channel_id=1, source_target_pairs={{0,8},{8,16},{16,24},{24,32},{32,40},{40,48},{48,56},{56,0},{1,9},... | collective-permute-start | bytes 86024 | tf_op jit(solution)/shard_map/ppermute | solution.py:41
  41.2 14.6 %collective-permute-start.3 = (f32[2,1,4096]{2,1,0:T(1,128)S(1)}, f32[2,1,4096]{2,1,0:T(1,128)S(1)}, u32[]{:S(2)}, u32[]{:S(2)}) collective-permute-start(f32[2,1,4096]{2,1,0:T(1,128)S(1)} %get-tuple-element.364), channel_id=1, source_target_pairs={{1,0},{2,1},{3,2},{4,3},{5,4},{6,5},{7,6},{8,7},{9,8},{10,9},{11,1... | collective-permute-start | bytes 98312 | tf_op jit(solution)/shard_map/ppermute | solution.py:43
  42.6 17.0 %collective-permute-start.2 = (f32[2,1,4096]{2,1,0:T(1,128)S(1)}, f32[2,1,4096]{2,1,0:T(1,128)S(1)}, u32[]{:S(2)}, u32[]{:S(2)}) collective-permute-start(f32[2,1,4096]{2,1,0:T(1,128)S(1)} %get-tuple-element.363), channel_id=1, source_target_pairs={{0,1},{1,2},{2,3},{3,4},{4,5},{5,6},{6,7},{7,8},{8,9},{9,10},{10,1... | collective-permute-start | bytes 98312 | tf_op jit(solution)/shard_map/ppermute | solution.py:41
  45.0 19.3 %collective-permute-start.11 = (f32[7,68,2]{2,1,0:T(8,128)S(1)}, f32[7,68,2]{2,1,0:T(8,128)}, u32[]{:S(2)}, u32[]{:S(2)}) collective-permute-start(f32[7,68,2]{2,1,0:T(8,128)S(1)} %get-tuple-element.326), channel_id=1, source_target_pairs={{1,0},{2,1},{3,2},{4,3},{5,4},{6,5},{7,6},{0,7},{9,8},{10,9},{11,1... | collective-permute-start | bytes 11432 | tf_op jit(solution)/shard_map/ppermute | solution.py:43
  46.5 17.9 %collective-permute-start.10 = (f32[7,68,2]{2,1,0:T(8,128)S(1)}, f32[7,68,2]{2,1,0:T(8,128)}, u32[]{:S(2)}, u32[]{:S(2)}) collective-permute-start(f32[7,68,2]{2,1,0:T(8,128)S(1)} %get-tuple-element.325), channel_id=1, source_target_pairs={{0,1},{1,2},{2,3},{3,4},{4,5},{5,6},{6,7},{7,0},{8,9},{9,10},{10,1... | collective-permute-start | bytes 11432 | tf_op jit(solution)/shard_map/ppermute | solution.py:41
  60.0 12.7 %collective-permute-start.5 = (f32[2,1,4096]{2,1,0:T(1,128)S(1)}, f32[2,1,4096]{2,1,0:T(1,128)S(1)}, u32[]{:S(2)}, u32[]{:S(2)}) collective-permute-start(f32[2,1,4096]{2,1,0:T(1,128)S(1)} %get-tuple-element.362), channel_id=1, source_target_pairs={{1,0},{2,1},{3,2},{4,3},{5,4},{6,5},{7,6},{8,7},{9,8},{10,9},{11,1... | collective-permute-start | bytes 98312 | tf_op jit(solution)/shard_map/ppermute | solution.py:43
  64.3 9.3 %collective-permute-start.4 = (f32[2,1,4096]{2,1,0:T(1,128)S(1)}, f32[2,1,4096]{2,1,0:T(1,128)S(1)}, u32[]{:S(2)}, u32[]{:S(2)}) collective-permute-start(f32[2,1,4096]{2,1,0:T(1,128)S(1)} %get-tuple-element.361), channel_id=1, source_target_pairs={{0,1},{1,2},{2,3},{3,4},{4,5},{5,6},{6,7},{7,8},{8,9},{9,10},{10,1... | collective-permute-start | bytes 98312 | tf_op jit(solution)/shard_map/ppermute | solution.py:41
  74.1 8.3 %collective-permute-start.7 = (f32[2,1,4096]{2,1,0:T(1,128)S(1)}, f32[2,1,4096]{2,1,0:T(1,128)S(1)}, u32[]{:S(2)}, u32[]{:S(2)}) collective-permute-start(f32[2,1,4096]{2,1,0:T(1,128)S(1)} %get-tuple-element.360), channel_id=1, source_target_pairs={{1,0},{2,1},{3,2},{4,3},{5,4},{6,5},{7,6},{8,7},{9,8},{10,9},{11,1... | collective-permute-start | bytes 98312 | tf_op jit(solution)/shard_map/ppermute | solution.py:43
  80.8 9.8 %collective-permute-start.6 = (f32[2,1,4096]{2,1,0:T(1,128)S(1)}, f32[2,1,4096]{2,1,0:T(1,128)S(1)}, u32[]{:S(2)}, u32[]{:S(2)}) collective-permute-start(f32[2,1,4096]{2,1,0:T(1,128)S(1)} %get-tuple-element.359), channel_id=1, source_target_pairs={{0,1},{1,2},{2,3},{3,4},{4,5},{5,6},{6,7},{7,8},{8,9},{9,10},{10,1... | collective-permute-start | bytes 98312 | tf_op jit(solution)/shard_map/ppermute | solution.py:41
  104.1 7.9 %collective-permute-start.14 = (f32[4,2,4096]{2,1,0:T(2,128)S(1)}, f32[4,2,4096]{2,1,0:T(2,128)S(1)}, u32[]{:S(2)}, u32[]{:S(2)}) collective-permute-start(f32[4,2,4096]{2,1,0:T(2,128)S(1)} %get-tuple-element.344), channel_id=1, source_target_pairs={{1,0},{2,1},{3,2},{4,3},{5,4},{6,5},{7,6},{8,7},{9,8},{10,9},{11,1... | collective-permute-start | bytes 393224 | tf_op jit(solution)/shard_map/ppermute | solution.py:43
  105.3 11.0 %collective-permute-start.13 = (f32[4,2,4096]{2,1,0:T(2,128)S(1)}, f32[4,2,4096]{2,1,0:T(2,128)S(1)}, u32[]{:S(2)}, u32[]{:S(2)}) collective-permute-start(f32[4,2,4096]{2,1,0:T(2,128)S(1)} %get-tuple-element.343), channel_id=1, source_target_pairs={{0,1},{1,2},{2,3},{3,4},{4,5},{5,6},{6,7},{7,8},{8,9},{9,10},{10,1... | collective-permute-start | bytes 393224 | tf_op jit(solution)/shard_map/ppermute | solution.py:41
  120.3 5.5 %collective-permute-start.16 = (f32[2,1,4096]{2,1,0:T(1,128)S(1)}, f32[2,1,4096]{2,1,0:T(1,128)S(1)}, u32[]{:S(2)}, u32[]{:S(2)}) collective-permute-start(f32[2,1,4096]{2,1,0:T(1,128)S(1)} %get-tuple-element.358), channel_id=1, source_target_pairs={{1,0},{2,1},{3,2},{4,3},{5,4},{6,5},{7,6},{8,7},{9,8},{10,9},{11,1... | collective-permute-start | bytes 98312 | tf_op jit(solution)/shard_map/ppermute | solution.py:43
  120.4 9.4 %collective-permute-start.15 = (f32[2,1,4096]{2,1,0:T(1,128)S(1)}, f32[2,1,4096]{2,1,0:T(1,128)S(1)}, u32[]{:S(2)}, u32[]{:S(2)}) collective-permute-start(f32[2,1,4096]{2,1,0:T(1,128)S(1)} %get-tuple-element.357), channel_id=1, source_target_pairs={{0,1},{1,2},{2,3},{3,4},{4,5},{5,6},{6,7},{7,8},{8,9},{9,10},{10,1... | collective-permute-start | bytes 98312 | tf_op jit(solution)/shard_map/ppermute | solution.py:41
  130.3 5.5 %collective-permute-start.18 = (f32[2,1,4096]{2,1,0:T(1,128)S(1)}, f32[2,1,4096]{2,1,0:T(1,128)S(1)}, u32[]{:S(2)}, u32[]{:S(2)}) collective-permute-start(f32[2,1,4096]{2,1,0:T(1,128)S(1)} %get-tuple-element.356), channel_id=1, source_target_pairs={{1,0},{2,1},{3,2},{4,3},{5,4},{6,5},{7,6},{8,7},{9,8},{10,9},{11,1... | collective-permute-start | bytes 98312 | tf_op jit(solution)/shard_map/ppermute | solution.py:43
  130.4 9.4 %collective-permute-start.17 = (f32[2,1,4096]{2,1,0:T(1,128)S(1)}, f32[2,1,4096]{2,1,0:T(1,128)S(1)}, u32[]{:S(2)}, u32[]{:S(2)}) collective-permute-start(f32[2,1,4096]{2,1,0:T(1,128)S(1)} %get-tuple-element.355), channel_id=1, source_target_pairs={{0,1},{1,2},{2,3},{3,4},{4,5},{5,6},{6,7},{7,8},{8,9},{9,10},{10,1... | collective-permute-start | bytes 98312 | tf_op jit(solution)/shard_map/ppermute | solution.py:41
  140.5 13.0 %collective-permute-start.19 = (f32[2,1,4096]{2,1,0:T(1,128)S(1)}, f32[2,1,4096]{2,1,0:T(1,128)S(1)}, u32[]{:S(2)}, u32[]{:S(2)}) collective-permute-start(f32[2,1,4096]{2,1,0:T(1,128)S(1)} %get-tuple-element.353), channel_id=1, source_target_pairs={{0,1},{1,2},{2,3},{3,4},{4,5},{5,6},{6,7},{7,8},{8,9},{9,10},{10,1... | collective-permute-start | bytes 98312 | tf_op jit(solution)/shard_map/ppermute | solution.py:41
  156.0 36.0 %all-to-all-start.2 = ((f32[8,5,1,8,512]{4,3,1,2,0:T(8,128)}), f32[8,5,1,8,512]{4,3,1,2,0:T(8,128)S(1)}, u32[]{:S(2)}, u32[]{:S(2)}) async-start(f32[8,5,1,8,512]{4,3,1,2,0:T(8,128)} %copy.57), calls=%async_computation.2 | async-start | bytes 1310720 | tf_op jit(solution)/shard_map/all_to_all | solution.py:19
  159.6 6.4 %collective-permute-start.21 = (f32[7,2,512]{2,1,0:T(2,128)S(1)}, f32[7,2,512]{2,1,0:T(2,128)S(1)}, u32[]{:S(2)}, u32[]{:S(2)}) collective-permute-start(f32[7,2,512]{2,1,0:T(2,128)S(1)} %get-tuple-element.327), channel_id=1, source_target_pairs={{0,8},{8,16},{16,24},{24,32},{32,40},{40,48},{48,56},{56,0},{1,9},... | collective-permute-start | bytes 86024 | tf_op jit(solution)/shard_map/ppermute | solution.py:41
  166.2 10.0 %collective-permute-start.24 = (f32[7,68,2]{2,1,0:T(8,128)S(1)}, f32[7,68,2]{2,1,0:T(8,128)S(1)}, u32[]{:S(2)}, u32[]{:S(2)}) collective-permute-start(f32[7,68,2]{2,1,0:T(8,128)S(1)} %get-tuple-element.324), channel_id=1, source_target_pairs={{1,0},{2,1},{3,2},{4,3},{5,4},{6,5},{7,6},{0,7},{9,8},{10,9},{11,1... | collective-permute-start | bytes 11432 | tf_op jit(solution)/shard_map/ppermute | solution.py:43
  171.8 12.7 %collective-permute-start.23 = (f32[7,68,2]{2,1,0:T(8,128)S(1)}, f32[7,68,2]{2,1,0:T(8,128)S(1)}, u32[]{:S(2)}, u32[]{:S(2)}) collective-permute-start(f32[7,68,2]{2,1,0:T(8,128)S(1)} %get-tuple-element.323), channel_id=1, source_target_pairs={{0,1},{1,2},{2,3},{3,4},{4,5},{5,6},{6,7},{7,0},{8,9},{9,10},{10,1... | collective-permute-start | bytes 11432 | tf_op jit(solution)/shard_map/ppermute | solution.py:41
  (6 other events, 18.0 us)
